TPU v7x, 32 devices: a whole 2x2x4 slice. The times are simulated.
32 devices in a mesh: pp: 4 (over y, x), cp: 4 (over z), tp: 2 (over core).
Axes of the slice: x: 2, y: 2, z: 4, core: 2. Of those that a mesh axis runs over, the one named last changes fastest.
Arguments:
- queries: bfloat16 [2048, 16384], P(('pp', 'cp'), 'tp'), may hold values from -12 to 12
- keys: bfloat16 [2048, 1024], P(('pp', 'cp'), 'tp'), may hold values from -12 to 12
- values: bfloat16 [2048, 1024], P(('pp', 'cp'), 'tp'), may hold values from -6 to 6
- pair_order: int32 [4, 4], replicated, may hold values from 0 to 3, each once within a row
- lengths: int32 [4, 2], replicated, may hold values from 128 to 256
- routes: int32 [4, 512, 1], P(None, 'cp'), may hold values from 0 to 7; in each aligned block of 128 rows (0 to 127, 128 to 255, ..., all dimensions but the last counted through in order) at most 32 rows name the same one
Outputs:
- rebalanced: bfloat16 [4096, 16384], P(('pp', 'cp', 'tp'))
Inputs may be any that keep to these rules, and one draw needn't show every extreme that they name: `routes`: at most 32 rows of one device's block name the same destination, and in some block one destination is named by exactly 32 rows.
All inputs are finite; a program needn't handle non-finite values.
Results may differ from a plain program's by a relative error of at most 0.003.
Values may be sent and summed in bfloat16 or wider, within the bound.
No kernel may reach another device: no remote copies, remote signals or barrier semaphores. Data moves between devices by JAX's collectives and lax.ppermute only.
A program may use at most 64 MiB of HBM per device.

v0:
```python
import jax
import jax.numpy as jnp
from jax import lax
from jax.sharding import PartitionSpec as P

HD = 128
masked_score = -1e30


def shifted(block, axis, distance):
    devices = range(lax.axis_size(axis))
    route = [((i - distance) % len(devices), i) for i in devices]
    return lax.ppermute(block, axis, route)


def pair_positions(pair_ids, block_len, cycle_size):
    offsets = jnp.arange(block_len, dtype=jnp.int32)
    first_half = pair_ids[:, None] * block_len + offsets[None, :]
    second_half = (2 * cycle_size - 1 - pair_ids)[:, None] * block_len + offsets[None, :]
    return jnp.concatenate([first_half, second_half], axis=1)


def dispatch_rows(attended, targets, dest_count, capacity):
    row_count = attended.shape[0]
    matches = targets[:, None] == jnp.arange(dest_count, dtype=jnp.int32)[None, :]
    row_ids = jnp.arange(row_count, dtype=jnp.int32)
    earlier = (row_ids[None, :] < row_ids[:, None]).astype(jnp.bfloat16)
    before = jnp.dot(earlier, matches.astype(jnp.bfloat16), preferred_element_type=jnp.float32)
    slot_index = jnp.sum(jnp.where(matches, before, 0.0), axis=1).astype(jnp.int32)
    slot_ids = jnp.arange(capacity, dtype=jnp.int32)
    picked_rows = jnp.logical_and(
        jnp.transpose(matches)[:, None, :], slot_index[None, None, :] == slot_ids[None, :, None]
    )
    selector = picked_rows.astype(jnp.bfloat16).reshape(dest_count * capacity, row_count)
    return jnp.dot(selector, attended, preferred_element_type=jnp.float32).astype(jnp.bfloat16)


def spread_rows(buffer, cycle_size, split_size, capacity, width):
    flat_buffer = buffer.reshape(cycle_size * split_size, capacity, width)
    moved = lax.all_to_all(flat_buffer, ("cp", "tp"), split_axis=0, concat_axis=0, tiled=True)
    moved = jnp.transpose(moved.reshape(cycle_size, split_size, capacity, width), (0, 2, 1, 3))
    return moved.reshape(cycle_size * capacity, split_size * width)


def arrange_rows(attended, routes, source, cycle_size, split_size):
    row_count, width = attended.shape
    dest_count = cycle_size * split_size
    capacity = 2 * row_count // dest_count
    targets = lax.dynamic_index_in_dim(routes, source, 0, keepdims=False)[:, 0]
    buffer = dispatch_rows(attended, targets, dest_count, capacity)
    buffer = buffer.reshape(cycle_size, split_size, capacity, width)
    return spread_rows(buffer, cycle_size, split_size, capacity, width)


def body(queries, keys, values, pair_order, lengths, routes):
    cycle_size = lax.axis_size("cp")
    split_size = lax.axis_size("tp")
    section = lax.axis_index("pp")
    place = lax.axis_index("cp")
    row_count = queries.shape[0]
    block_len = row_count // 4
    width = queries.shape[1]
    group_count = keys.shape[1] // HD
    group_size = width // keys.shape[1]
    score_scale = HD ** (-0.5)
    order_row = lax.dynamic_index_in_dim(pair_order, section, 0, keepdims=False)
    own_pair = lax.dynamic_index_in_dim(order_row, place, 0, keepdims=True)
    query_pos = pair_positions(own_pair, block_len, cycle_size).reshape(2 * block_len)
    limits = lax.dynamic_index_in_dim(lengths, section, 0, keepdims=False)
    query_rows = queries.reshape(2, 2 * block_len, group_count, group_size, HD)
    stat_shape = (2, 2 * block_len, group_count, group_size)
    start_state = (
        jnp.full(stat_shape, masked_score, jnp.float32),
        jnp.zeros(stat_shape, jnp.float32),
        jnp.zeros(stat_shape + (HD,), jnp.float32),
    )
    state = start_state
    key_piece = lax.all_gather(keys, "cp", axis=0, tiled=True)
    value_piece = lax.all_gather(values, "cp", axis=0, tiled=True)
    shard_count = key_piece.shape[0] // row_count
    first_shard = jnp.int32(0) // row_count
    for base in range(0, shard_count, 4):
        block = min(4, shard_count - base)
        key_block = key_piece[base * row_count : (base + block) * row_count].reshape(
            block, 2, 2 * block_len, group_count, HD
        )
        value_block = value_piece[base * row_count : (base + block) * row_count].reshape(
            block, 2, 2 * block_len, group_count, HD
        )
        shard_ids = first_shard + base + jnp.arange(block, dtype=jnp.int32)
        key_pos = pair_positions(order_row[shard_ids], block_len, cycle_size).reshape(
            block * 2 * block_len
        )
        allowed = jnp.logical_and(
            key_pos[None, None, :] <= query_pos[None, :, None],
            key_pos[None, None, :] < limits[:, None, None],
        )
        allowed = allowed[:, :, None, None, :]
        scores = jnp.einsum(
            "sqgrd,nskgd->sqgrnk", query_rows, key_block, preferred_element_type=jnp.float32
        )
        scores = scores.reshape(stat_shape + (block * 2 * block_len,)) * score_scale
        running_max, running_total, running_sum = state
        block_max = jnp.max(jnp.where(allowed, scores, masked_score), axis=4)
        new_max = jnp.maximum(running_max, block_max)
        weights = jnp.where(allowed, jnp.exp(scores - new_max[..., None]), 0.0)
        carry_factor = jnp.exp(running_max - new_max)
        running_total = running_total * carry_factor + jnp.sum(weights, axis=4)
        shaped = weights.astype(jnp.bfloat16).reshape(stat_shape + (block, 2 * block_len))
        running_sum = running_sum * carry_factor[..., None] + jnp.einsum(
            "sqgrnk,nskgd->sqgrd", shaped, value_block, preferred_element_type=jnp.float32
        )
        state = (new_max, running_total, running_sum)
    attended = (state[2] / state[1][..., None]).astype(jnp.bfloat16).reshape(row_count, width)
    arranged = arrange_rows(attended, routes, section, cycle_size, split_size)
    return shifted(arranged, "pp", 1)


def solution(mesh):
    placed = (
        P(("pp", "cp"), "tp"),
        P(("pp", "cp"), "tp"),
        P(("pp", "cp"), "tp"),
        P(),
        P(),
        P(None, "cp", None),
    )
    return jax.shard_map(
        body, mesh=mesh, in_specs=placed, out_specs=P(("pp", "cp", "tp"), None), check_vma=False
    )
```

profile of v0, /device:TPU:0, one launch (start us, length us, event | category | flops | bytes accessed | tf_op | source)
XLA Modules:
  0.0 287.3 jit_solution(959507155664328261)
XLA Ops:
  0.0 0.7 copy-done
  0.7 0.1 fusion.9
  0.9 0.7 fusion.14
  1.6 1.3 dynamic_slice.18
  4.1 0.6 gather_fusion
  4.8 0.9 dynamic-slice_reduce_fusion
  6.1 2.2 copy.30
  8.3 17.4 %all_gather.6 = bf16[512,512]{1,0:T(8,128)(2,1)S(1)} all-gather(bf16[128,512]{1,0:T(8,128)(2,1)S(1)} %copy-done.2), channel_id=1, replica_groups=mesh['pp'=4,'cp'=4,'tp'=2] {'cp'}, dimensions={0}, use_global_device_ids=true | all-gather | bytes 655360 | tf_op jit(solution)/shard_map/all_gather | solution.py:78
  25.8 0.1 broadcast_and_fusion
  25.9 5.5 %fusion = (f32[2,64,4,16]{1,3,2,0:T(8,128)S(1)}, f32[2,4,4,64,64,16]{4,3,5,2,1,0:T(8,128)S(1)}) fusion(pred[2,64,4,64]{1,3,2,0:T(8,128)(4,1)S(1)} %broadcast_and_fusion, bf16[2,64,4,16,128,1]{4,3,2,1,0,5:T(8,128)(2,1)S(1)} %bitcast.52, bf16[4,2,64,4,128,1]{4,3,2,1,0,5:T(4,128)(2,1)S(1)} %bitcast.54), kind=kOutput, calls=%fused_computation.3 | convolution fusion | flops 543154176 | bytes 11075584 | tf_op jit(solution)/shard_map/sqgrd,nskgd->sqgrnk/dot_general | solution.py:99
  31.4 6.2 %fusion.3 = (f32[2,64,4,16]{1,3,2,0:T(8,128)S(1)}, bf16[2,64,4,16,4,64]{1,5,3,4,2,0:T(8,128)(2,1)}) fusion(f32[2,4,4,64,64,16]{4,3,5,2,1,0:T(8,128)S(1)} %get-tuple-element.12, f32[2,64,4,16]{1,3,2,0:T(8,128)S(1)} %broadcast_maximum_fusion, pred[2,64,4,64]{1,3,2,0:T(8,128)(4,1)S(1)} %broadcast_and_fusion), kind=kLoop, calls=%fused_computation.6 | loop fusion | flops 10477568 | bytes 12681216 | tf_op jit(solution)/shard_map/reduce_sum | solution.py:108
  37.8 0.1 copy.17
  38.0 17.2 %copy.15 = bf16[2,64,4,16,4,64]{5,3,4,1,2,0:T(8,128)(2,1)} copy(bf16[2,64,4,16,4,64]{1,5,3,4,2,0:T(8,128)(2,1)} %get-tuple-element.6) | data formatting | bytes 8388608 | tf_op jit(solution)/shard_map/convert_element_type | solution.py:109
  55.2 16.2 %all_gather.7 = bf16[512,512]{1,0:T(8,128)(2,1)S(1)} all-gather(bf16[128,512]{1,0:T(8,128)(2,1)S(1)} %copy-done.3), channel_id=1, replica_groups=mesh['pp'=4,'cp'=4,'tp'=2] {'cp'}, dimensions={0}, use_global_device_ids=true | all-gather | bytes 655360 | tf_op jit(solution)/shard_map/all_gather | solution.py:79
  71.6 5.7 %fusion.6 = bf16[2,64,4,16,128]{4,3,1,2,0:T(8,128)(2,1)S(1)} fusion(bf16[2,64,4,16,4,64]{5,3,4,1,2,0:T(8,128)(2,1)} %copy.15, f32[2,64,4,16]{3,1,2,0:T(8,128)S(1)} %copy.17, f32[2,64,4,16]{3,1,2,0:T(8,128)S(1)} %copy.14, bf16[4,2,64,4,128,1]{4,3,2,1,0,5:T(4,128)(2,1)S(1)} %bitcast.56), kind=kOutput, calls=%fused_computation.11 | convolution fusion | flops 540016640 | bytes 6881280 | tf_op jit(solution)/shard_map/sqgrnk,nskgd->sqgrd/dot_general | solution.py:110
  77.3 1.9 copy.18
  79.2 2.8 reshape.237
  82.1 1.2 convolution_convert_fusion
  83.3 97.9 %all_to_all.5 = bf16[8,32,8192]{2,1,0:T(8,128)(2,1)S(1)} all-to-all(bf16[8,32,8192]{2,1,0:T(8,128)(2,1)S(1)} %bitcast.49), channel_id=1, replica_groups=mesh['pp'=4,'cp'=4,'tp'=2] {'cp','tp'}, dimensions={0} | all-to-all | bytes 8388608 | tf_op jit(solution)/shard_map/all_to_all | solution.py:40
  181.2 6.4 %copy.19 = bf16[4,2,32,8192]{3,1,2,0:T(2,128)(2,1)} copy(bf16[4,2,32,8192]{3,2,1,0:T(8,128)(2,1)S(1)} %bitcast.50) | data formatting | bytes 8388608 | tf_op jit(solution)/shard_map/reshape | solution.py:41
  187.6 4.8 %copy.31 = bf16[16,8,2,8192]{3,1,2,0:T(8,128)(2,1)S(1)} copy(bf16[16,8,2,8192]{3,2,1,0:T(2,128)(2,1)} %bitcast.51) | data formatting | bytes 8388608
  192.4 1.6 collective-permute-start
  194.0 91.3 %collective-permute-done = bf16[128,16384]{1,0:T(8,128)(2,1)S(1)} collective-permute-done((bf16[128,16384]{1,0:T(8,128)(2,1)S(1)}, bf16[128,16384]{1,0:T(8,128)(2,1)S(1)}, u32[]{:S(2)}, u32[]{:S(2)}) %collective-permute-start) | collective-permute-done | bytes 4194336 | tf_op jit(solution)/shard_map/ppermute | solution.py:13
  285.3 2.0 copy.45
  (26 shorter events, 0.9 us)
Async XLA Ops:
  0.0 0.7 copy-start
  0.0 8.3 %copy-start.2 = (bf16[128,512]{1,0:T(8,128)(2,1)S(1)}, bf16[128,512]{1,0:T(8,128)(2,1)}, u32[]{:S(2)}) copy-start(bf16[128,512]{1,0:T(8,128)(2,1)} %param.7) | copy-start | bytes 393220
  38.0 17.2 %copy-start.3 = (bf16[128,512]{1,0:T(8,128)(2,1)S(1)}, bf16[128,512]{1,0:T(8,128)(2,1)}, u32[]{:S(2)}) copy-start(bf16[128,512]{1,0:T(8,128)(2,1)} %param.8) | copy-start | bytes 393220
  192.4 94.9 %copy-start.1 = (s32[4,128,1]{1,2,0:T(1,128)S(1)}, s32[4,128,1]{1,2,0:T(1,128)}, u32[]{:S(2)}) copy-start(s32[4,128,1]{1,2,0:T(1,128)} %param.11) | copy-start | bytes 6148
  192.4 92.9 %collective-permute-start = (bf16[128,16384]{1,0:T(8,128)(2,1)S(1)}, bf16[128,16384]{1,0:T(8,128)(2,1)S(1)}, u32[]{:S(2)}, u32[]{:S(2)}) collective-permute-start(bf16[128,16384]{1,0:T(8,128)(2,1)S(1)} %bitcast.53), channel_id=1, source_target_pairs={{24,0},{0,8},{8,16},{16,24},{25,1},{1,9},{9,17},{17,25},{26,2},{2,... | collective-permute-start | bytes 12582920 | tf_op jit(solution)/shard_map/ppermute | solution.py:13
where the time goes:
time: 288 us; the launch traced here: 287 us
  blocking collectives  131 us (45%)
  waiting for transfers between devices  91.3 us (32%)
  local copies, waits for them, and re-layouts  42 us (15%)
  matrix products  12.6 us (4%)
  other arithmetic  6.85 us (2%)
    all_to_all x1, blocking collectives, spread_rows(): lax.all_to_all(flat_buffer, ('cp', 'tp'), split_axis=0, concat_axis=0, ti...  97.9 us
    ppermute x1, waiting for transfers between devices, shifted(): return lax.ppermute(block, axis, route)  91.3 us
    all_gather x1, blocking collectives, body(): key_piece = lax.all_gather(keys, 'cp', axis=0, tiled=True)  17.4 us
    convert_element_type x1, local copies, waits for them, and re-layouts, body(): weights.astype(jnp.bfloat16).reshape(stat_shape + (block, 2 * block_len))  17.2 us
    all_gather x1, blocking collectives, body(): value_piece = lax.all_gather(values, 'cp', axis=0, tiled=True)  16.2 us
    unnamed x11, local copies, waits for them, and re-layouts  9.69 us
    reshape x1, local copies, waits for them, and re-layouts, spread_rows(): moved.reshape(cycle_size, split_size, capacity, width)  6.38 us
    reduce_sum x1, other arithmetic, body(): running_total = running_total * carry_factor + jnp.sum(weights, axis=4)  6.22 us
  transfers between devices with their start and end apart: 1, of which 1 were waited for; matrix products, arithmetic and copies ran while one was open for 0% of the time, Pallas kernels for 0%

commit v1 on v0

--- a/solution.py
+++ b/solution.py
@@ -5,6 +5,20 @@
 
 HD = 128
 masked_score = -1e30
+
+
+def order_digits_by_axis(panel):
+    nodes = lax.axis_size("cp")
+    part_now = panel
+    lower = [(hop_no - 1, hop_no) for hop_no in range(1, nodes)] + [(nodes - 1, 0)]
+    slots = [part_now]
+    for _ in [*range(nodes - 1)]:
+        part_now = lax.ppermute(part_now, "cp", lower)
+        slots += [part_now]
+    then = jnp.roll(
+        jnp.concatenate([*reversed(slots)], 0), (lax.axis_index("cp") + 1) * part_now.shape[0], 0
+    )
+    return then
 
 
 def shifted(block, axis, distance):
@@ -76,7 +90,7 @@
     )
     state = start_state
     key_piece = lax.all_gather(keys, "cp", axis=0, tiled=True)
-    value_piece = lax.all_gather(values, "cp", axis=0, tiled=True)
+    value_piece = order_digits_by_axis(values)
     shard_count = key_piece.shape[0] // row_count
     first_shard = jnp.int32(0) // row_count
     for base in range(0, shard_count, 4):

time: 288 us -> 268 us (0.931)
  blocking collectives: 131 us -> 112 us
  local copies, waits for them, and re-layouts: 42 us -> 24.7 us
  waiting for transfers between devices: 91.3 us -> 104 us
  starting transfers between devices: 1.55 us -> 5.15 us
    convert_element_type x1 -> x0, local copies, waits for them, and re-layouts: 17.2 us -> none  [body(): weights.astype(jnp.bfloat16).reshape(stat_shape + (block, 2 * block_len))]
    all_gather x1 -> x0, blocking collectives: 16.2 us -> none  [body(): value_piece = lax.all_gather(values, 'cp', axis=0, tiled=True)]
    ppermute x0 -> x3, waiting for transfers between devices: none -> 13 us  [order_digits_by_axis(): part_now = lax.ppermute(part_now, 'cp', lower)]
    ppermute x0 -> x3, starting transfers between devices: none -> 3.6 us  [order_digits_by_axis(): part_now = lax.ppermute(part_now, 'cp', lower)]
    unnamed x11 -> x16, local copies, waits for them, and re-layouts: 9.69 us -> 9.08 us
  transfers between devices with their start and end apart: 1 -> 4, of which waited for: 1 -> 3; matrix products, arithmetic and copies ran while one was open for 0% -> 7% of each run, Pallas kernels for 0% -> 0%
where the time goes in v1:
time: 268 us
  blocking collectives  112 us (42%)
  waiting for transfers between devices  104 us (39%)
  local copies, waits for them, and re-layouts  24.7 us (9%)
  matrix products  13.6 us (5%)
  other arithmetic  6.84 us (3%)
  starting transfers between devices  5.15 us (2%)
    all_to_all x1, blocking collectives, spread_rows(): lax.all_to_all(flat_buffer, ('cp', 'tp'), split_axis=0, concat_axis=0, ti...  96.5 us
    ppermute x1, waiting for transfers between devices, shifted(): return lax.ppermute(block, axis, route)  91.3 us
    all_gather x1, blocking collectives, body(): key_piece = lax.all_gather(keys, 'cp', axis=0, tiled=True)  15.3 us
    ppermute x3, waiting for transfers between devices, order_digits_by_axis(): part_now = lax.ppermute(part_now, 'cp', lower)  13 us
    unnamed x16, local copies, waits for them, and re-layouts  9.08 us
    dot_general x1, matrix products, body(): jnp.einsum('sqgrnk,nskgd->sqgrd', shaped, value_block, preferred_element_...  6.76 us
    reshape x1, local copies, waits for them, and re-layouts, spread_rows(): moved.reshape(cycle_size, split_size, capacity, width)  6.38 us
    reduce_sum x1, other arithmetic, body(): running_total = running_total * carry_factor + jnp.sum(weights, axis=4)  6.2 us
  transfers between devices with their start and end apart: 4, of which 3 were waited for; matrix products, arithmetic and copies ran while one was open for 7% of the time, Pallas kernels for 0%

profile of v1, /device:TPU:0, one launch (start us, length us, event | category | flops | bytes accessed | tf_op | source)
XLA Modules:
  0.0 268.1 jit_solution(13775427035968339375)
XLA Ops:
  0.0 3.0 %collective-permute-start = (bf16[128,512]{1,0:T(8,128)(2,1)}, bf16[128,512]{1,0:T(8,128)(2,1)S(1)}, u32[]{:S(2)}, u32[]{:S(2)}) collective-permute-start(bf16[128,512]{1,0:T(8,128)(2,1)} %param.8), channel_id=1, source_target_pairs={{0,2},{2,4},{4,6},{6,0},{1,3},{3,5},{5,7},{7,1},{8,10},{10,12},{12... | collective-permute-start | bytes 393224 | tf_op jit(solution)/shard_map/ppermute | solution.py:16
  3.0 0.7 fusion.18
  3.7 1.3 dynamic_slice.22
  6.3 0.6 gather_fusion
  6.9 0.9 dynamic-slice_reduce_fusion
  8.2 2.2 copy.28
  10.4 15.3 %all_gather.3 = bf16[512,512]{1,0:T(8,128)(2,1)S(1)} all-gather(bf16[128,512]{1,0:T(8,128)(2,1)S(1)} %copy-done.2), channel_id=1, replica_groups=mesh['pp'=4,'cp'=4,'tp'=2] {'cp'}, dimensions={0}, use_global_device_ids=true | all-gather | bytes 655360 | tf_op jit(solution)/shard_map/all_gather | solution.py:92
  25.9 0.1 broadcast_and_fusion
  26.0 5.5 %fusion = (f32[2,64,4,16]{1,3,2,0:T(8,128)S(1)}, f32[2,4,4,64,64,16]{4,3,5,2,1,0:T(8,128)S(1)}) fusion(pred[2,64,4,64]{1,3,2,0:T(8,128)(4,1)S(1)} %broadcast_and_fusion, bf16[2,64,4,16,128,1]{4,3,2,1,0,5:T(8,128)(2,1)S(1)} %bitcast.51, bf16[4,2,64,4,128,1]{4,3,2,1,0,5:T(4,128)(2,1)S(1)} %bitcast.53), kind=kOutput, calls=%fused_computation.3 | convolution fusion | flops 543154176 | bytes 11075584 | tf_op jit(solution)/shard_map/sqgrd,nskgd->sqgrnk/dot_general | solution.py:113
  31.6 6.2 %fusion.3 = (f32[2,64,4,16]{1,3,2,0:T(8,128)S(1)}, bf16[2,64,4,16,4,64]{1,5,3,4,2,0:T(8,128)(2,1)}) fusion(f32[2,4,4,64,64,16]{4,3,5,2,1,0:T(8,128)S(1)} %get-tuple-element.12, f32[2,64,4,16]{1,3,2,0:T(8,128)S(1)} %broadcast_maximum_fusion, pred[2,64,4,64]{1,3,2,0:T(8,128)(4,1)S(1)} %broadcast_and_fusion), kind=kLoop, calls=%fused_computation.6 | loop fusion | flops 10477568 | bytes 12681216 | tf_op jit(solution)/shard_map/reduce_sum | solution.py:122
  37.8 0.1 fusion.13
  38.0 0.6 collective-permute-start.1
  38.6 6.2 %collective-permute-done.1 = bf16[128,512]{1,0:T(8,128)(2,1)S(1)} collective-permute-done((bf16[128,512]{1,0:T(8,128)(2,1)S(1)}, bf16[128,512]{1,0:T(8,128)(2,1)S(1)}, u32[]{:S(2)}, u32[]{:S(2)}) %collective-permute-start.1) | collective-permute-done | bytes 131104 | tf_op jit(solution)/shard_map/ppermute | solution.py:16
  44.9 6.7 %collective-permute-done.2 = bf16[128,512]{1,0:T(8,128)(2,1)S(1)} collective-permute-done((bf16[128,512]{1,0:T(8,128)(2,1)S(1)}, bf16[128,512]{1,0:T(8,128)(2,1)S(1)}, u32[]{:S(2)}, u32[]{:S(2)}) %collective-permute-start.2) | collective-permute-done | bytes 131104 | tf_op jit(solution)/shard_map/ppermute | solution.py:16
  52.0 6.8 %fusion.8 = bf16[2,64,4,16,128]{4,1,3,2,0:T(8,128)(2,1)S(1)} fusion(bf16[2,64,4,16,4,64]{1,5,3,4,2,0:T(8,128)(2,1)} %get-tuple-element.6, f32[2,64,4,16]{1,3,2,0:T(8,128)S(1)} %get-tuple-element.8, f32[2,64,4,16]{1,3,2,0:T(8,128)S(1)} %get-tuple-element.7, bf16[4,2,64,4,128,1]{4,3,2,1,0,5:T(4,128)(2,1)S(1)} %bitcast.55), kind=kOutput, calls=%fused_computation.13 | convolution fusion | flops 540016640 | bytes 6881280 | tf_op jit(solution)/shard_map/sqgrnk,nskgd->sqgrd/dot_general | solution.py:124
  58.7 2.7 copy.14
  61.4 2.8 %reshape.237 = bf16[128,8192]{1,0:T(8,128)(2,1)S(1)} reshape(bf16[2,64,4,16,128]{4,3,2,1,0:T(8,128)(2,1)} %copy.14) | data formatting | bytes 4194304 | tf_op jit(solution)/shard_map/reshape | solution.py:128
  64.2 1.2 convolution_convert_fusion
  65.5 96.5 %all_to_all.5 = bf16[8,32,8192]{2,1,0:T(8,128)(2,1)S(1)} all-to-all(bf16[8,32,8192]{2,1,0:T(8,128)(2,1)S(1)} %bitcast.48), channel_id=1, replica_groups=mesh['pp'=4,'cp'=4,'tp'=2] {'cp','tp'}, dimensions={0} | all-to-all | bytes 8388608 | tf_op jit(solution)/shard_map/all_to_all | solution.py:54
  162.0 6.4 %copy.15 = bf16[4,2,32,8192]{3,1,2,0:T(2,128)(2,1)} copy(bf16[4,2,32,8192]{3,2,1,0:T(8,128)(2,1)S(1)} %bitcast.49) | data formatting | bytes 8388608 | tf_op jit(solution)/shard_map/reshape | solution.py:55
  168.4 4.8 %copy.29 = bf16[16,8,2,8192]{3,1,2,0:T(8,128)(2,1)S(1)} copy(bf16[16,8,2,8192]{3,2,1,0:T(2,128)(2,1)} %bitcast.50) | data formatting | bytes 8388608
  173.2 1.5 collective-permute-start.3
  174.7 91.3 %collective-permute-done.3 = bf16[128,16384]{1,0:T(8,128)(2,1)S(1)} collective-permute-done((bf16[128,16384]{1,0:T(8,128)(2,1)S(1)}, bf16[128,16384]{1,0:T(8,128)(2,1)S(1)}, u32[]{:S(2)}, u32[]{:S(2)}) %collective-permute-start.3) | collective-permute-done | bytes 4194336 | tf_op jit(solution)/shard_map/ppermute | solution.py:27
  266.1 2.0 copy.54
  (35 shorter events, 0.9 us)
Async XLA Ops:
  0.0 37.8 %copy-start = (s32[4,128,1]{1,2,0:T(1,128)S(1)}, s32[4,128,1]{1,2,0:T(1,128)}, u32[]{:S(2)}) copy-start(s32[4,128,1]{1,2,0:T(1,128)} %param.11) | copy-start | bytes 6148
  0.0 10.4 %copy-start.2 = (bf16[128,512]{1,0:T(8,128)(2,1)S(1)}, bf16[128,512]{1,0:T(8,128)(2,1)}, u32[]{:S(2)}) copy-start(bf16[128,512]{1,0:T(8,128)(2,1)} %param.7) | copy-start | bytes 393220
  0.0 38.0 %collective-permute-start = (bf16[128,512]{1,0:T(8,128)(2,1)}, bf16[128,512]{1,0:T(8,128)(2,1)S(1)}, u32[]{:S(2)}, u32[]{:S(2)}) collective-permute-start(bf16[128,512]{1,0:T(8,128)(2,1)} %param.8), channel_id=1, source_target_pairs={{0,2},{2,4},{4,6},{6,0},{1,3},{3,5},{5,7},{7,1},{8,10},{10,12},{12... | collective-permute-start | bytes 393224 | tf_op jit(solution)/shard_map/ppermute | solution.py:16
  31.6 20.1 %copy-start.1 = (bf16[128,512]{1,0:T(8,128)(2,1)S(1)}, bf16[128,512]{1,0:T(8,128)(2,1)}, u32[]{:S(2)}) copy-start(bf16[128,512]{1,0:T(8,128)(2,1)} %param.8) | copy-start | bytes 393220
  38.0 6.8 %collective-permute-start.1 = (bf16[128,512]{1,0:T(8,128)(2,1)S(1)}, bf16[128,512]{1,0:T(8,128)(2,1)S(1)}, u32[]{:S(2)}, u32[]{:S(2)}) collective-permute-start(bf16[128,512]{1,0:T(8,128)(2,1)S(1)} %collective-permute-done), channel_id=1, source_target_pairs={{0,2},{2,4},{4,6},{6,0},{1,3},{3,5},{5,7},{7,1},{8,10},{10,12},{12... | collective-permute-start | bytes 393224 | tf_op jit(solution)/shard_map/ppermute | solution.py:16
  44.9 6.8 %collective-permute-start.2 = (bf16[128,512]{1,0:T(8,128)(2,1)S(1)}, bf16[128,512]{1,0:T(8,128)(2,1)S(1)}, u32[]{:S(2)}, u32[]{:S(2)}) collective-permute-start(bf16[128,512]{1,0:T(8,128)(2,1)S(1)} %collective-permute-done.1), channel_id=1, source_target_pairs={{0,2},{2,4},{4,6},{6,0},{1,3},{3,5},{5,7},{7,1},{8,10},{10,12},{12... | collective-permute-start | bytes 393224 | tf_op jit(solution)/shard_map/ppermute | solution.py:16
  173.2 92.9 %collective-permute-start.3 = (bf16[128,16384]{1,0:T(8,128)(2,1)S(1)}, bf16[128,16384]{1,0:T(8,128)(2,1)S(1)}, u32[]{:S(2)}, u32[]{:S(2)}) collective-permute-start(bf16[128,16384]{1,0:T(8,128)(2,1)S(1)} %bitcast.52), channel_id=1, source_target_pairs={{24,0},{0,8},{8,16},{16,24},{25,1},{1,9},{9,17},{17,25},{26,2},{2,... | collective-permute-start | bytes 12582920 | tf_op jit(solution)/shard_map/ppermute | solution.py:27
